TPU v7x, 512 devices: a whole 4x8x8 slice. The times are simulated.
512 devices in a mesh: blk: 32 (over y, x), head: 16 (over z, core).
Axes of the slice: x: 4, y: 8, z: 8, core: 2. Of those that a mesh axis runs over, the one named last changes fastest.
Arguments:
- tokens: bfloat16 [2048, 4096], P('blk', 'head'), may hold values from -6 to 6
- queries: bfloat16 [2048, 36864], P('blk', 'head'), may hold values from -600 to 600
- latents: bfloat16 [2048, 576], P('blk'), may hold values from -6 to 6
- value_up: bfloat16 [64, 512, 128], P('head'), may hold values from -0.25 to 0.25
- out_proj: bfloat16 [8192, 4096], P('head', 'blk'), may hold values from -0.09375 to 0.09375
- expert_ids: int32 [2048, 8], P('blk'), may hold values from 0 to 31, all different within a row; in each aligned block of 64 rows (0 to 63, 64 to 127, ...) at most 20 rows name the same one
- expert_gates: float32 [2048, 8], P('blk'), may hold values from 0.05 to 0.5
- w_gate: bfloat16 [32, 4096, 2048], P('blk', None, 'head'), may hold values from -0.09375 to 0.09375
- w_up: bfloat16 [32, 4096, 2048], P('blk', None, 'head'), may hold values from -0.09375 to 0.09375
- w_down: bfloat16 [32, 2048, 4096], P('blk', None, 'head'), may hold values from -0.125 to 0.125
Outputs:
- result: bfloat16 [2048, 4096], P('blk', 'head')
Inputs may be any that keep to these rules, and one draw needn't show every extreme that they name: `expert_ids`: among the tokens of one index of blk (aligned blocks of 64 rows) at most 20 choose one expert, and some expert is chosen by exactly 20 of them; the experts of one row differ.
All inputs are finite; a program needn't handle non-finite values.
Results may differ from a plain program's by a relative error of at most 0.013.
Values may be sent and summed in bfloat16 or wider, within the bound.
No kernel may reach another device: no remote copies, remote signals or barrier semaphores. Data moves between devices by JAX's collectives and lax.ppermute only.
A program may use at most 64 MiB of HBM per device.

v0:
```python
import jax
import jax.numpy as jnp
from jax import lax
from jax.sharding import PartitionSpec as P

D = 4096
LAT = 512
ROPE = 64
QKNOPE = 128
EXPERTS = 32
CAP = 20


def per_device(
    tokens, queries, latents, value_up, out_proj, expert_ids, expert_gates, w_gate, w_up, w_down
):
    row_count = tokens.shape[0]
    heads_here = value_up.shape[0]
    first_row = lax.axis_index("blk") * row_count
    score_scale = (QKNOPE + ROPE) ** (-0.5)
    query_heads = queries.reshape(row_count, heads_here, LAT + ROPE)
    query_pos = first_row + jnp.arange(row_count, dtype=jnp.int32)
    last_query = first_row + row_count - 1
    start_state = (
        jnp.full((row_count, heads_here), -1e30, jnp.float32),
        jnp.zeros((row_count, heads_here), jnp.float32),
        jnp.zeros((row_count, heads_here, LAT), jnp.float32),
    )
    segment = lax.all_gather(latents, "blk", axis=0, tiled=True)

    def compute(state_in):
        running_max, denominator, accumulated = state_in
        key_count = segment.shape[0]
        scores = (
            jnp.einsum("qhc,kc->qhk", query_heads, segment, preferred_element_type=jnp.float32)
            * score_scale
        )
        key_pos = jnp.arange(key_count, dtype=jnp.int32)
        allowed = (key_pos[None, :] <= query_pos[:, None])[:, None, :]
        scores = jnp.where(allowed, scores, -1e30)
        new_max = jnp.maximum(running_max, jnp.max(scores, axis=2))
        exp_weights = jnp.where(allowed, jnp.exp(scores - new_max[:, :, None]), 0.0)
        denominator = jnp.sum(exp_weights, axis=2)
        accumulated = jnp.einsum(
            "qhk,kc->qhc",
            exp_weights.astype(jnp.bfloat16),
            segment[:, :LAT],
            preferred_element_type=jnp.float32,
        )
        return (new_max, denominator, accumulated)

    def keep(state_in):
        return state_in

    running_max, denominator, accumulated = lax.cond(
        jnp.int32(0) <= last_query, compute, keep, start_state
    )
    context = (accumulated / denominator[:, :, None]).astype(jnp.bfloat16)
    lifted = jnp.einsum(
        "qhc,hcv->qhv", context, value_up, preferred_element_type=jnp.float32
    ).astype(jnp.bfloat16)
    lifted = lifted.reshape(row_count, heads_here * value_up.shape[2])
    partial_out = jnp.dot(
        lifted,
        lax.all_gather(out_proj, "blk", axis=1, tiled=True),
        preferred_element_type=jnp.float32,
    )
    attended = lax.psum_scatter(
        partial_out.astype(jnp.bfloat16), "head", scatter_dimension=1, tiled=True
    ).astype(jnp.float32)
    mid_state = (tokens.astype(jnp.float32) + attended).astype(jnp.bfloat16)
    mid_wide = mid_state.astype(jnp.float32)
    squares = lax.psum(jnp.sum(mid_wide * mid_wide, axis=1), "head")
    normed = (mid_wide * lax.rsqrt(squares / D + 1e-06)[:, None]).astype(jnp.bfloat16)
    flat_ids = expert_ids.reshape(-1)
    choose_count = expert_ids.shape[1]
    onehot_ids = (flat_ids[:, None] == jnp.arange(EXPERTS, dtype=jnp.int32)[None, :]).astype(
        jnp.int32
    )
    earlier = jnp.cumsum(onehot_ids, axis=0) - onehot_ids
    ranks = jnp.sum(earlier * onehot_ids, axis=1)
    slot_ids = flat_ids * CAP + ranks
    slot_hits = jnp.arange(EXPERTS * CAP, dtype=jnp.int32)[:, None] == slot_ids[None, :]
    select = jnp.sum(
        slot_hits.astype(jnp.bfloat16).reshape(EXPERTS * CAP, row_count, choose_count), axis=2
    )
    combine = jnp.sum(
        jnp.where(slot_hits, expert_gates.reshape(-1)[None, :], 0.0).reshape(
            EXPERTS * CAP, row_count, choose_count
        ),
        axis=2,
    )
    outgoing = (
        jnp.dot(select, normed, preferred_element_type=jnp.float32)
        .astype(jnp.bfloat16)
        .reshape(EXPERTS, CAP, normed.shape[1])
    )
    incoming = lax.all_to_all(outgoing, "blk", split_axis=0, concat_axis=1, tiled=True)
    contract_segment = lax.all_gather(incoming, "head", axis=2, tiled=True)
    gate_add = jnp.einsum(
        "esd,edf->esf", contract_segment, w_gate, preferred_element_type=jnp.float32
    )
    up_add = jnp.einsum("esd,edf->esf", contract_segment, w_up, preferred_element_type=jnp.float32)
    activation = (jax.nn.silu(gate_add) * up_add).astype(jnp.bfloat16)
    expert_out = jnp.einsum(
        "esf,efd->esd",
        lax.all_gather(activation, "head", axis=2, tiled=True),
        w_down,
        preferred_element_type=jnp.float32,
    ).astype(jnp.bfloat16)
    returned = lax.all_to_all(expert_out, "blk", split_axis=1, concat_axis=0, tiled=True)
    returned_wide = returned.reshape(EXPERTS * CAP, returned.shape[2]).astype(jnp.float32)
    routed = jnp.einsum("sr,sd->rd", combine, returned_wide, precision=lax.Precision.HIGHEST)
    return (mid_wide + routed).astype(jnp.bfloat16)


def solution(mesh):
    placed = (
        P("blk", "head"),
        P("blk", "head"),
        P("blk", None),
        P("head", None, None),
        P("head", "blk"),
        P("blk", None),
        P("blk", None),
        P("blk", None, "head"),
        P("blk", None, "head"),
        P("blk", None, "head"),
    )
    return jax.shard_map(
        per_device, mesh=mesh, in_specs=placed, out_specs=P("blk", "head"), check_vma=False
    )
```

profile of v0, /device:TPU:8, one launch (start us, length us, event | category | flops | bytes accessed | tf_op | source)
XLA Modules:
  0.0 443.7 jit_solution(13091606071966224623)
XLA Ops:
  6.5 0.7 all-gather.6.cloned.1.call-update
  7.3 0.0 all-gather.8.cloned.1.call-start
  7.3 0.7 all-gather.8.cloned.1.call-update
  8.0 0.0 reduce-scatter.2.cloned.1.call-start
  8.1 90.0 %all-gather.6.cloned.1.call-done = bf16[2048,576]{1,0:T(8,128)(2,1)} async-done(((bf16[64,576]{1,0:T(8,128)(2,1)}), bf16[2048,576]{1,0:T(8,128)(2,1)}) %all-gather.6.cloned.1.call-update) | async-done | bytes 2359312 | tf_op jit(solution)/shard_map/all_gather | solution.py:29
  98.1 6.0 %conditional.1 = (f32[64,4]{0,1:T(4,128)S(1)}, f32[64,4,512]{2,0,1:T(8,128)S(1)}) conditional(s32[]{:T(128)} %convert_element_type.66, () %tuple.13, (s32[]{:T(128)}, s32[64]{0:T(128)S(1)}, bf16[64,2304]{1,0:T(8,128)(2,1)}, bf16[2048,576]{1,0:T(8,128)(2,1)}) %tuple.14), branch_computations={%region_0.0_spmd, %region_1.4_spmd} | conditional | flops 1145700096 | bytes 22126384 | solution.py:55
  98.1 0.1 iota_compare_fusion
  98.2 1.4 reshape.109
  99.6 3.1 fusion.44
  102.7 0.8 fusion.2
  103.5 0.5 fusion.6
  104.0 0.3 fusion.25
  104.3 83.3 %all-gather.8.cloned.1.call-done = bf16[512,4096]{1,0:T(8,128)(2,1)} async-done(((bf16[512,128]{1,0:T(8,128)(2,1)}), bf16[512,4096]{1,0:T(8,128)(2,1)}) %all-gather.8.cloned.1.call-update) | async-done | bytes 4194320 | tf_op jit(solution)/shard_map/all_gather | solution.py:65
  187.6 3.8 convolution_convert_fusion
  191.5 0.0 all-gather.10.cloned.1.call-start
  191.6 0.1 copy.60
  191.7 0.1 eq.45
  191.8 0.1 eq.41
  191.9 1.2 reduce-window.6
  193.0 0.2 slice_reduce_fusion
  193.3 0.1 fusion.38
  193.4 0.1 reduce_sum.51
  193.5 0.1 copy.63
  193.6 0.1 copy.64
  193.7 0.5 fusion.30
  194.1 58.6 %reduce-scatter.2.cloned.1.call-done = bf16[64,256]{1,0:T(8,128)(2,1)} async-done(((bf16[64,4096]{1,0:T(8,128)(2,1)}), bf16[64,256]{1,0:T(8,128)(2,1)}) %reduce-scatter.2.cloned.1.call-update) | async-done | bytes 32784 | tf_op jit(solution)/shard_map/reduce_scatter | solution.py:68
  252.7 0.9 fusion.34
  253.6 23.6 %psum.7 = f32[64]{0:T(128)S(1)} all-reduce(f32[64]{0:T(128)S(1)} %fusion.34), channel_id=1, replica_groups=mesh['blk'=32,'head'=16] {'head'}, use_global_device_ids=true, to_apply=%region_11.12 | all-reduce | flops 64 | bytes 512 | tf_op jit(solution)/shard_map/psum | solution.py:73
  277.2 1.1 convolution_convert_fusion.2
  278.3 0.1 reshape.121
  278.3 24.3 %all_to_all.21 = bf16[32,20,256]{2,1,0:T(8,128)(2,1)S(1)} all-to-all(bf16[32,20,256]{2,1,0:T(8,128)(2,1)S(1)} %reshape.121), channel_id=1, replica_groups=mesh['blk'=32,'head'=16] {'blk'}, dimensions={0} | all-to-all | bytes 655360 | tf_op jit(solution)/shard_map/all_to_all | solution.py:98
  302.7 0.8 all_to_all.7
  303.5 0.0 all-gather.12.cloned.1.call-start
  303.6 49.1 %all-gather.10.cloned.1.call-done = bf16[1,640,4096]{2,1,0:T(8,128)(2,1)} async-done(((bf16[1,640,256]{2,1,0:T(8,128)(2,1)}), bf16[1,640,4096]{2,1,0:T(8,128)(2,1)}) %all-gather.10.cloned.1.call-update) | async-done | bytes 5242896 | tf_op jit(solution)/shard_map/all_gather | solution.py:99
  352.6 4.1 fusion.15
  356.8 3.4 fusion.22
  360.2 45.0 %all-gather.12.cloned.1.call-done = bf16[640,2048]{1,0:T(8,128)(2,1)} async-done(((bf16[640,128]{1,0:T(8,128)(2,1)}), bf16[640,2048]{1,0:T(8,128)(2,1)}) %all-gather.12.cloned.1.call-update) | async-done | bytes 2621456 | tf_op jit(solution)/shard_map/all_gather | solution.py:107
  405.3 2.6 fusion.18
  407.9 0.5 copy.86
  408.4 0.5 broadcast.62
  408.9 2.7 reduce.3
  411.6 0.8 reshape.133
  412.4 9.8 %all-to-all-start.1 = ((bf16[32,2,2560]{2,1,0:T(2,128)(2,1)}), bf16[32,2,2560]{2,1,0:T(2,128)(2,1)S(1)}, u32[]{:S(2)}, u32[]{:S(2)}) async-start(bf16[32,2,2560]{2,1,0:T(2,128)(2,1)} %reshape.133), calls=%async_computation.2 | async-start | bytes 655360 | tf_op jit(solution)/shard_map/all_to_all | solution.py:111
  422.3 0.1 copy.65
  422.3 0.5 select_reduce_fusion
  422.8 13.2 %all-to-all-done.1 = bf16[32,2,2560]{2,1,0:T(2,128)(2,1)S(1)} async-done(((bf16[32,2,2560]{2,1,0:T(2,128)(2,1)}), bf16[32,2,2560]{2,1,0:T(2,128)(2,1)S(1)}, u32[]{:S(2)}, u32[]{:S(2)}) %all-to-all-start.1) | async-done | bytes 327712 | tf_op jit(solution)/shard_map/all_to_all | solution.py:111
  436.0 0.3 reshape.134
  436.3 0.9 fusion.26
  (30 shorter events, 0.2 us)
Async XLA Ops:
  6.5 398.7 %copy-start = (bf16[1,2048,256]{2,1,0:T(8,128)(2,1)S(1)}, bf16[1,2048,256]{2,1,0:T(8,128)(2,1)}, u32[]{:S(2)}) copy-start(bf16[1,2048,256]{2,1,0:T(8,128)(2,1)} %param.21) | copy-start | bytes 3145732
  6.5 91.5 %all-gather.6.cloned.1.call-start = ((), (), s32[]{:S(2)}) async-start(), calls=%async_computation.3 | async-start | bytes 2703360 | tf_op jit(solution)/shard_map/all_gather | solution.py:29
  7.3 180.4 %all-gather.8.cloned.1.call-start = ((), (), s32[]{:S(2)}) async-start(), calls=%async_computation.4 | async-start | bytes 4325376 | tf_op jit(solution)/shard_map/all_gather | solution.py:65
  8.0 244.7 %reduce-scatter.2.cloned.1.call-start = ((), (), s32[]{:S(2)}) async-start(), calls=%async_computation.5 | async-start | bytes 557056 | tf_op jit(solution)/shard_map/reduce_scatter | solution.py:68
  98.1 6.0 %copy-start.8 = (bf16[4,512,128]{2,1,0:T(8,128)(2,1)S(1)}, bf16[4,512,128]{2,1,0:T(8,128)(2,1)}, u32[]{:S(2)}) copy-start(bf16[4,512,128]{2,1,0:T(8,128)(2,1)} %param.15) | copy-start | bytes 1572868
  99.6 3.1 copy-start.6
  104.3 87.3 %copy-start.3 = (s32[64,8]{0,1:T(8,128)S(1)}, s32[64,8]{0,1:T(8,128)}, u32[]{:S(2)}) copy-start(s32[64,8]{0,1:T(8,128)} %param.17) | copy-start | bytes 6148
  104.3 148.4 %copy-start.1 = (bf16[64,256]{1,0:T(8,128)(2,1)S(1)}, bf16[64,256]{1,0:T(8,128)(2,1)}, u32[]{:S(2)}) copy-start(bf16[64,256]{1,0:T(8,128)(2,1)} %param.12) | copy-start | bytes 98308
  191.5 161.1 %copy-start.7 = (bf16[1,4096,128]{2,1,0:T(8,128)(2,1)S(1)}, bf16[1,4096,128]{2,1,0:T(8,128)(2,1)}, u32[]{:S(2)}) copy-start(bf16[1,4096,128]{2,1,0:T(8,128)(2,1)} %param.19) | copy-start | bytes 3145732
  191.5 161.1 %all-gather.10.cloned.1.call-start = ((), (), s32[]{:S(2)}) async-start(), calls=%async_computation.6 | async-start | bytes 5570560 | tf_op jit(solution)/shard_map/all_gather | solution.py:99
  303.5 101.7 %all-gather.12.cloned.1.call-start = ((), (), s32[]{:S(2)}) async-start(), calls=%async_computation.7 | async-start | bytes 2785280 | tf_op jit(solution)/shard_map/all_gather | solution.py:107
  352.6 4.1 copy-start.5
  407.8 14.4 %copy-start.4 = (f32[64,8]{0,1:T(8,128)S(1)}, f32[64,8]{0,1:T(8,128)}, u32[]{:S(2)}) copy-start(f32[64,8]{0,1:T(8,128)} %param.18) | copy-start | bytes 6148
  407.9 28.5 %copy-start.2 = (bf16[64,256]{1,0:T(8,128)(2,1)S(1)}, bf16[64,256]{1,0:T(8,128)(2,1)}, u32[]{:S(2)}) copy-start(bf16[64,256]{1,0:T(8,128)(2,1)} %reduce-scatter.2.cloned.1.call-done) | copy-start | bytes 98308
  412.4 23.6 %all-to-all-start.1 = ((bf16[32,2,2560]{2,1,0:T(2,128)(2,1)}), bf16[32,2,2560]{2,1,0:T(2,128)(2,1)S(1)}, u32[]{:S(2)}, u32[]{:S(2)}) async-start(bf16[32,2,2560]{2,1,0:T(2,128)(2,1)} %reshape.133), calls=%async_computation.2 | async-start | bytes 655360 | tf_op jit(solution)/shard_map/all_to_all | solution.py:111
Sparse Core Ops, SparseCore 0:
  10.5 87.5 all-gather.5
  101.1 86.5 all-gather.7
  191.6 61.0 reduce-scatter.1
  303.6 48.9 all-gather.9
  360.3 44.8 all-gather.11
where the time goes:
time: 444 us
  waiting for transfers between devices  341 us (77%)
  blocking collectives  47.9 us (11%)
  matrix products  20.1 us (5%)
  between operations  13.3 us (3%)
  starting transfers between devices  10 us (2%)
  other arithmetic  6.52 us (1%)
  local copies, waits for them, and re-layouts  5.17 us (1%)
    all_gather x1, waiting for transfers between devices, per_device(): segment = lax.all_gather(latents, 'blk', axis=0, tiled=True)  90 us
    all_gather x1, waiting for transfers between devices, per_device(): lax.all_gather(out_proj, 'blk', axis=1, tiled=True)  83.3 us
    reduce_scatter x1, waiting for transfers between devices, per_device(): lax.psum_scatter(partial_out.astype(jnp.bfloat16), 'head', scatter_dimens...  58.6 us
    all_gather x1, waiting for transfers between devices, per_device(): contract_segment = lax.all_gather(incoming, 'head', axis=2, tiled=True)  49.1 us
    all_gather x1, waiting for transfers between devices, per_device(): lax.all_gather(activation, 'head', axis=2, tiled=True)  45 us
    all_to_all x1, blocking collectives, per_device(): lax.all_to_all(outgoing, 'blk', split_axis=0, concat_axis=1, tiled=True)  24.3 us
    psum x1, blocking collectives, per_device(): squares = lax.psum(jnp.sum(mid_wide * mid_wide, axis=1), 'head')  23.6 us
    all_to_all x1, waiting for transfers between devices, per_device(): lax.all_to_all(expert_out, 'blk', split_axis=1, concat_axis=0, tiled=True)  13.2 us
  transfers between devices with their start and end apart: 6, of which 6 were waited for; matrix products, arithmetic and copies ran while one was open for 2% of the time, Pallas kernels for 0%

commit v1 on v0

--- a/solution.py
+++ b/solution.py
@@ -26,7 +26,9 @@
         jnp.zeros((row_count, heads_here), jnp.float32),
         jnp.zeros((row_count, heads_here, LAT), jnp.float32),
     )
-    segment = lax.all_gather(latents, "blk", axis=0, tiled=True)
+    segment = jnp.concatenate(
+        lax.all_to_all(jnp.stack([latents] * lax.axis_size("blk")), "blk", 0, 0), axis=0
+    )
 
     def compute(state_in):
         running_max, denominator, accumulated = state_in

time: 444 us -> 382 us (0.86)
  waiting for transfers between devices: 341 us -> 264 us
  starting transfers between devices: 10 us -> 20.5 us
    all_gather x1 -> x0, waiting for transfers between devices: 90 us -> none  [per_device(): segment = lax.all_gather(latents, 'blk', axis=0, tiled=True)]
    all_to_all x0 -> x1, waiting for transfers between devices: none -> 65.8 us  [per_device(): lax.all_to_all(jnp.stack([latents] * lax.axis_size('blk')), 'blk', 0, 0)]
    all_gather x1, waiting for transfers between devices: 83.3 us -> 31.9 us  [per_device(): lax.all_gather(out_proj, 'blk', axis=1, tiled=True)]
    all_to_all x0 -> x1, starting transfers between devices: none -> 10.3 us  [per_device(): lax.all_to_all(jnp.stack([latents] * lax.axis_size('blk')), 'blk', 0, 0)]
  transfers between devices with their start and end apart: 6 -> 6, of which waited for: 6 -> 6; matrix products, arithmetic and copies ran while one was open for 2% -> 3% of each run, Pallas kernels for 0% -> 0%
where the time goes in v1:
time: 382 us; the launch traced here: 381 us
  waiting for transfers between devices  264 us (69%)
  blocking collectives  47.9 us (13%)
  matrix products  21.6 us (6%)
  starting transfers between devices  20.5 us (5%)
  between operations  13.3 us (3%)
  local copies, waits for them, and re-layouts  7 us (2%)
  other arithmetic  6.51 us (2%)
    all_to_all x1, waiting for transfers between devices, per_device(): lax.all_to_all(jnp.stack([latents] * lax.axis_size('blk')), 'blk', 0, 0)  65.8 us
    reduce_scatter x1, waiting for transfers between devices, per_device(): lax.psum_scatter(partial_out.astype(jnp.bfloat16), 'head', scatter_dimens...  58.8 us
    all_gather x1, waiting for transfers between devices, per_device(): contract_segment = lax.all_gather(incoming, 'head', axis=2, tiled=True)  48.7 us
    all_gather x1, waiting for transfers between devices, per_device(): lax.all_gather(activation, 'head', axis=2, tiled=True)  45 us
    all_gather x1, waiting for transfers between devices, per_device(): lax.all_gather(out_proj, 'blk', axis=1, tiled=True)  31.9 us
    all_to_all x1, blocking collectives, per_device(): lax.all_to_all(outgoing, 'blk', split_axis=0, concat_axis=1, tiled=True)  24.3 us
    psum x1, blocking collectives, per_device(): squares = lax.psum(jnp.sum(mid_wide * mid_wide, axis=1), 'head')  23.6 us
    all_to_all x1, waiting for transfers between devices, per_device(): lax.all_to_all(expert_out, 'blk', split_axis=1, concat_axis=0, tiled=True)  13.2 us
  transfers between devices with their start and end apart: 6, of which 6 were waited for; matrix products, arithmetic and copies ran while one was open for 3% of the time, Pallas kernels for 0%

profile of v1, /device:TPU:8, one launch (start us, length us, event | category | flops | bytes accessed | tf_op | source)
XLA Modules:
  0.0 381.0 jit_solution(10287543382940387727)
XLA Ops:
  6.5 0.7 all-gather.5.cloned.1.call-update
  7.3 2.8 stack.2
  10.0 10.3 %all-to-all-start = ((bf16[32,64,576]{2,1,0:T(8,128)(2,1)}), bf16[32,64,576]{2,1,0:T(8,128)(2,1)}, u32[]{:S(2)}, u32[]{:S(2)}) async-start(bf16[32,64,576]{2,1,0:T(8,128)(2,1)} %stack.2), calls=%async_computation | async-start | bytes 5242880 | tf_op jit(solution)/shard_map/all_to_all | solution.py:30
  20.4 0.0 reduce-scatter.2.cloned.1.call-start
  20.5 65.8 %all-to-all-done = bf16[32,64,576]{2,1,0:T(8,128)(2,1)} async-done(((bf16[32,64,576]{2,1,0:T(8,128)(2,1)}), bf16[32,64,576]{2,1,0:T(8,128)(2,1)}, u32[]{:S(2)}, u32[]{:S(2)}) %all-to-all-start) | async-done | bytes 2359328 | tf_op jit(solution)/shard_map/all_to_all | solution.py:30
  86.3 6.5 %conditional.1 = (f32[64,4]{0,1:T(4,128)S(1)}, f32[64,4,512]{2,0,1:T(8,128)S(1)}) conditional(s32[]{:T(128)} %convert_element_type.66, () %tuple.13, (s32[]{:T(128)}, s32[64]{0:T(128)S(1)}, bf16[64,2304]{1,0:T(8,128)(2,1)S(1)}, bf16[32,64,576]{2,1,0:T(8,128)(2,1)}) %tuple.26), branch_computations={%region_0.0_spmd, %region_1.4_spmd} | conditional | flops 1145700096 | bytes 12688148 | solution.py:57
  86.3 0.1 iota_compare_fusion
  86.4 0.4 reshape.114
  86.8 2.9 fusion.41
  89.7 2.4 fusion.1
  92.2 0.5 fusion.3
  92.7 0.3 fusion.22
  93.0 31.9 %all-gather.5.cloned.1.call-done = bf16[512,4096]{1,0:T(8,128)(2,1)} async-done(((bf16[512,128]{1,0:T(8,128)(2,1)}), bf16[512,4096]{1,0:T(8,128)(2,1)}) %all-gather.5.cloned.1.call-update) | async-done | bytes 4194320 | tf_op jit(solution)/shard_map/all_gather | solution.py:67
  124.9 3.8 %convolution_convert_fusion = bf16[64,4096]{1,0:T(8,128)(2,1)} fusion(bf16[512,4096]{1,0:T(8,128)(2,1)} %all-gather.5.cloned.1.call-done, bf16[4,8,8,128]{3,2,1,0:T(8,128)(2,1)S(1)} %fusion.22), kind=kOutput, calls=%fused_computation.19 | convolution fusion | flops 268697600 | bytes 4784128 | tf_op jit(solution)/shard_map/dot_general | solution.py:65
  128.7 0.0 all-gather.7.cloned.1.call-start
  128.8 0.1 copy.60
  128.9 0.1 eq.45
  129.0 0.1 eq.41
  129.1 1.2 reduce-window.6
  130.3 0.2 slice_reduce_fusion
  130.5 0.1 fusion.35
  130.6 0.1 reduce_sum.51
  130.7 0.1 copy.63
  130.8 0.1 copy.64
  130.9 0.5 fusion.27
  131.4 58.8 %reduce-scatter.2.cloned.1.call-done = bf16[64,256]{1,0:T(8,128)(2,1)} async-done(((bf16[64,4096]{1,0:T(8,128)(2,1)}), bf16[64,256]{1,0:T(8,128)(2,1)}) %reduce-scatter.2.cloned.1.call-update) | async-done | bytes 32784 | tf_op jit(solution)/shard_map/reduce_scatter | solution.py:70
  190.2 0.9 fusion.31
  191.1 23.6 %psum.7 = f32[64]{0:T(128)S(1)} all-reduce(f32[64]{0:T(128)S(1)} %fusion.31), channel_id=1, replica_groups=mesh['blk'=32,'head'=16] {'head'}, use_global_device_ids=true, to_apply=%region_11.12 | all-reduce | flops 64 | bytes 512 | tf_op jit(solution)/shard_map/psum | solution.py:75
  214.7 1.1 convolution_convert_fusion.2
  215.7 0.1 reshape.127
  215.8 24.3 %all_to_all.26 = bf16[32,20,256]{2,1,0:T(8,128)(2,1)S(1)} all-to-all(bf16[32,20,256]{2,1,0:T(8,128)(2,1)S(1)} %reshape.127), channel_id=1, replica_groups=mesh['blk'=32,'head'=16] {'blk'}, dimensions={0} | all-to-all | bytes 655360 | tf_op jit(solution)/shard_map/all_to_all | solution.py:100
  240.2 0.8 all_to_all.10
  241.0 0.2 all-gather.9.cloned.1.call-start
  241.2 48.7 %all-gather.7.cloned.1.call-done = bf16[1,640,4096]{2,1,0:T(8,128)(2,1)} async-done(((bf16[1,640,256]{2,1,0:T(8,128)(2,1)}), bf16[1,640,4096]{2,1,0:T(8,128)(2,1)}) %all-gather.7.cloned.1.call-update) | async-done | bytes 5242896 | tf_op jit(solution)/shard_map/all_gather | solution.py:101
  289.9 4.1 %fusion.12 = f32[640,128]{1,0:T(8,128)S(1)} fusion(bf16[1,640,4096]{2,1,0:T(8,128)(2,1)} %all-gather.7.cloned.1.call-done, bf16[1,4096,128]{2,1,0:T(8,128)(2,1)S(1)} %copy-done.7), kind=kOutput, calls=%fused_computation.17 | convolution fusion | flops 671088640 | bytes 6619136 | tf_op jit(solution)/shard_map/esd,edf->esf/dot_general | solution.py:102
  294.1 3.4 fusion.19
  297.5 45.0 %all-gather.9.cloned.1.call-done = bf16[640,2048]{1,0:T(8,128)(2,1)} async-done(((bf16[640,128]{1,0:T(8,128)(2,1)}), bf16[640,2048]{1,0:T(8,128)(2,1)}) %all-gather.9.cloned.1.call-update) | async-done | bytes 2621456 | tf_op jit(solution)/shard_map/all_gather | solution.py:109
  342.5 2.6 fusion.15
  345.1 0.5 copy.86
  345.6 0.5 broadcast.64
  346.2 2.7 reduce.3
  348.9 0.8 reshape.139
  349.7 9.8 %all-to-all-start.2 = ((bf16[32,2,2560]{2,1,0:T(2,128)(2,1)}), bf16[32,2,2560]{2,1,0:T(2,128)(2,1)S(1)}, u32[]{:S(2)}, u32[]{:S(2)}) async-start(bf16[32,2,2560]{2,1,0:T(2,128)(2,1)} %reshape.139), calls=%async_computation.3 | async-start | bytes 655360 | tf_op jit(solution)/shard_map/all_to_all | solution.py:113
  359.5 0.1 copy.65
  359.6 0.5 select_reduce_fusion
  360.1 13.2 %all-to-all-done.2 = bf16[32,2,2560]{2,1,0:T(2,128)(2,1)S(1)} async-done(((bf16[32,2,2560]{2,1,0:T(2,128)(2,1)}), bf16[32,2,2560]{2,1,0:T(2,128)(2,1)S(1)}, u32[]{:S(2)}, u32[]{:S(2)}) %all-to-all-start.2) | async-done | bytes 327712 | tf_op jit(solution)/shard_map/all_to_all | solution.py:113
  373.3 0.3 reshape.140
  373.6 0.9 fusion.23
  (30 shorter events, 0.2 us)
Async XLA Ops:
  6.5 336.0 %copy-start = (bf16[1,2048,256]{2,1,0:T(8,128)(2,1)S(1)}, bf16[1,2048,256]{2,1,0:T(8,128)(2,1)}, u32[]{:S(2)}) copy-start(bf16[1,2048,256]{2,1,0:T(8,128)(2,1)} %param.21) | copy-start | bytes 3145732
  6.5 118.4 %all-gather.5.cloned.1.call-start = ((), (), s32[]{:S(2)}) async-start(), calls=%async_computation.4 | async-start | bytes 4325376 | tf_op jit(solution)/shard_map/all_gather | solution.py:67
  10.0 76.2 %copy-start.3 = (bf16[64,2304]{1,0:T(8,128)(2,1)S(1)}, bf16[64,2304]{1,0:T(8,128)(2,1)}, u32[]{:S(2)}) copy-start(bf16[64,2304]{1,0:T(8,128)(2,1)} %param.13) | copy-start | bytes 884740
  10.0 76.2 %all-to-all-start = ((bf16[32,64,576]{2,1,0:T(8,128)(2,1)}), bf16[32,64,576]{2,1,0:T(8,128)(2,1)}, u32[]{:S(2)}, u32[]{:S(2)}) async-start(bf16[32,64,576]{2,1,0:T(8,128)(2,1)} %stack.2), calls=%async_computation | async-start | bytes 5242880 | tf_op jit(solution)/shard_map/all_to_all | solution.py:30
  20.4 169.8 %reduce-scatter.2.cloned.1.call-start = ((), (), s32[]{:S(2)}) async-start(), calls=%async_computation.5 | async-start | bytes 557056 | tf_op jit(solution)/shard_map/reduce_scatter | solution.py:70
  86.3 6.5 %copy-start.8 = (bf16[4,512,128]{2,1,0:T(8,128)(2,1)S(1)}, bf16[4,512,128]{2,1,0:T(8,128)(2,1)}, u32[]{:S(2)}) copy-start(bf16[4,512,128]{2,1,0:T(8,128)(2,1)} %param.15) | copy-start | bytes 1572868
  93.0 35.8 %copy-start.4 = (s32[64,8]{0,1:T(8,128)S(1)}, s32[64,8]{0,1:T(8,128)}, u32[]{:S(2)}) copy-start(s32[64,8]{0,1:T(8,128)} %param.17) | copy-start | bytes 6148
  93.0 97.2 %copy-start.1 = (bf16[64,256]{1,0:T(8,128)(2,1)S(1)}, bf16[64,256]{1,0:T(8,128)(2,1)}, u32[]{:S(2)}) copy-start(bf16[64,256]{1,0:T(8,128)(2,1)} %param.12) | copy-start | bytes 98308
  128.7 161.2 %copy-start.7 = (bf16[1,4096,128]{2,1,0:T(8,128)(2,1)S(1)}, bf16[1,4096,128]{2,1,0:T(8,128)(2,1)}, u32[]{:S(2)}) copy-start(bf16[1,4096,128]{2,1,0:T(8,128)(2,1)} %param.19) | copy-start | bytes 3145732
  128.7 161.2 %all-gather.7.cloned.1.call-start = ((), (), s32[]{:S(2)}) async-start(), calls=%async_computation.6 | async-start | bytes 5570560 | tf_op jit(solution)/shard_map/all_gather | solution.py:101
  241.0 101.5 %all-gather.9.cloned.1.call-start = ((), (), s32[]{:S(2)}) async-start(), calls=%async_computation.7 | async-start | bytes 2785280 | tf_op jit(solution)/shard_map/all_gather | solution.py:109
  289.9 4.1 %copy-start.6 = (bf16[1,640,4096]{2,1,0:T(8,128)(2,1)S(1)}, bf16[1,640,4096]{2,1,0:T(8,128)(2,1)}, u32[]{:S(2)}) copy-start(bf16[1,640,4096]{2,1,0:T(8,128)(2,1)} %all-gather.7.cloned.1.call-done) | copy-start | bytes 15728644
  345.1 14.4 %copy-start.5 = (f32[64,8]{0,1:T(8,128)S(1)}, f32[64,8]{0,1:T(8,128)}, u32[]{:S(2)}) copy-start(f32[64,8]{0,1:T(8,128)} %param.18) | copy-start | bytes 6148
  345.1 28.5 %copy-start.2 = (bf16[64,256]{1,0:T(8,128)(2,1)S(1)}, bf16[64,256]{1,0:T(8,128)(2,1)}, u32[]{:S(2)}) copy-start(bf16[64,256]{1,0:T(8,128)(2,1)} %reduce-scatter.2.cloned.1.call-done) | copy-start | bytes 98308
  349.7 23.6 %all-to-all-start.2 = ((bf16[32,2,2560]{2,1,0:T(2,128)(2,1)}), bf16[32,2,2560]{2,1,0:T(2,128)(2,1)S(1)}, u32[]{:S(2)}, u32[]{:S(2)}) async-start(bf16[32,2,2560]{2,1,0:T(2,128)(2,1)} %reshape.139), calls=%async_computation.3 | async-start | bytes 655360 | tf_op jit(solution)/shard_map/all_to_all | solution.py:113
Sparse Core Ops, SparseCore 0:
  10.4 114.4 all-gather.4
  128.9 61.2 reduce-scatter.1
  241.1 48.7 all-gather.6
  297.6 44.8 all-gather.8
